TPU v7x, 32 devices: a whole 2x2x4 slice. The times are simulated.
32 devices in a mesh: groups: 2 (over y), points: 4 (over z), centers: 4 (over x, core).
Axes of the slice: x: 2, y: 2, z: 4, core: 2. Of those that a mesh axis runs over, the one named last changes fastest.
Arguments:
- train_points: bfloat16 [8192, 512], P(('groups', 'points')), parts along dimension 0, may hold values from -6 to 6
- saved_preds: float32 [8192, 128], P(('groups', 'points')), parts along dimension 0, may hold values from -6 to 6
- targets: float32 [8192, 128], P(('groups', 'points')), parts along dimension 0, may hold values from -6 to 6
- huber_delta: float32 [256], P('groups'), parts along dimension 0, may hold values from 0.3 to 3
- center_pos: bfloat16 [16384, 512], P(('groups', 'points', 'centers')), parts along dimension 0, may hold values from -6 to 6
- coefficients: bfloat16 [16384, 128], P(('groups', 'points', 'centers')), parts along dimension 0, may hold values from -0.8984375 to 0.8984375
- spread: bfloat16 [16384], P(('groups', 'points', 'centers')), parts along dimension 0, may hold values from 0.5 to 2
Outputs:
- grad_centers: float32 [16384, 512], P(('groups', 'points', 'centers')), parts along dimension 0
- grad_coef: float32 [16384, 128], P(('groups', 'points', 'centers')), parts along dimension 0
There are 2 independent parts, one for each index of `groups`. A program takes and returns all parts, laid end to end along the dimension named above; each array names one. Nothing has to cross between parts.
All inputs are finite; a program needn't handle non-finite values.
Results may differ from a plain program's by a relative error of at most 0.0003.
Values may be sent and summed in bfloat16 or wider, within the bound.
No kernel may reach another device: no remote copies, remote signals or barrier semaphores. Data moves between devices by JAX's collectives and lax.ppermute only.
A program may use at most 64 MiB of HBM per device.

v0:
```python
import jax
import jax.numpy as jnp
from jax import lax
from jax.sharding import PartitionSpec as P


def per_device(train_points, saved_preds, targets, huber_delta, center_pos, coefficients, spread):
    n_points, in_width = train_points.shape
    whole_pos, whole_coef, whole_rates = (
        lax.all_gather(center_pos, "points", axis=0, tiled=True),
        lax.all_gather(coefficients, "points", axis=0, tiled=True),
        lax.all_gather(spread, "points", axis=0, tiled=True),
    )
    center_sq = jnp.sum(jnp.square(whole_pos.astype(jnp.float32)), axis=1)
    rates = whole_rates.astype(jnp.float32)
    panel_width = whole_pos.shape[0]
    out_width = whole_coef.shape[1]
    block_rows = min(512, n_points)
    block_count = n_points // block_rows
    point_blocks = train_points.reshape(block_count, block_rows, in_width)

    def kernel_of(row_block):
        point_sq = jnp.sum(jnp.square(row_block.astype(jnp.float32)), axis=1)
        cross = lax.dot_general(
            row_block, whole_pos, (((1,), (1,)), ((), ())), preferred_element_type=jnp.float32
        )
        dist = point_sq[:, None] + center_sq[None, :] - 2.0 * cross
        return jnp.exp(-rates[None, :] * dist / in_width).astype(jnp.bfloat16)

    kernels = lax.map(kernel_of, point_blocks)
    partial_pred = jnp.dot(
        kernels.reshape(n_points, panel_width), whole_coef, preferred_element_type=jnp.float32
    )
    panel_pred = lax.psum(partial_pred, "centers")
    residual = panel_pred + saved_preds - targets
    cotangent = (residual / jnp.sqrt(1.0 + jnp.square(residual / huber_delta[None, :]))).astype(
        jnp.bfloat16
    )
    cot_blocks = cotangent.reshape(block_count, block_rows, out_width)

    def coef_term(kernel, cot_block):
        return lax.dot_general(
            kernel, cot_block, (((0,), (0,)), ((), ())), preferred_element_type=jnp.float32
        )

    def moment_terms(kernel, cot_block, row_block):
        mixing = lax.dot_general(
            cot_block, whole_coef, (((1,), (1,)), ((), ())), preferred_element_type=jnp.float32
        )
        weights = (kernel.astype(jnp.float32) * mixing).astype(jnp.bfloat16)
        totals = jnp.sum(weights.astype(jnp.float32), axis=0)
        moment = lax.dot_general(
            weights, row_block, (((0,), (0,)), ((), ())), preferred_element_type=jnp.float32
        )
        return (moment, totals)

    zero_coef = jnp.zeros((panel_width, out_width), jnp.float32)
    zero_moment = jnp.zeros((panel_width, in_width), jnp.float32)
    zero_totals = jnp.zeros((panel_width,), jnp.float32)

    def coef_pass(coef_acc, inputs):
        row_block, stored, cot_block = inputs
        return (coef_acc + coef_term(stored, cot_block), None)

    coef_acc, _ = lax.scan(coef_pass, zero_coef, (point_blocks, kernels, cot_blocks))
    grad_coef = lax.psum_scatter(coef_acc, "points", scatter_dimension=0, tiled=True)

    def moment_pass(totals, inputs):
        moment_acc, totals_acc = totals
        row_block, stored, cot_block = inputs
        moment, row_sum = moment_terms(stored, cot_block, row_block)
        return ((moment_acc + moment, totals_acc + row_sum), None)

    (moment_acc, totals_acc), _ = lax.scan(
        moment_pass, (zero_moment, zero_totals), (point_blocks, kernels, cot_blocks)
    )
    own_moment, own_totals = (
        lax.psum_scatter(moment_acc, "points", scatter_dimension=0, tiled=True),
        lax.psum_scatter(totals_acc, "points", scatter_dimension=0, tiled=True),
    )
    own_rates = spread.astype(jnp.float32)
    grad_centers = (2.0 * own_rates / in_width)[:, None] * (
        own_moment - own_totals[:, None] * center_pos.astype(jnp.float32)
    )
    return (grad_centers, grad_coef)


def solution(mesh):
    return jax.shard_map(
        per_device,
        mesh=mesh,
        in_specs=(
            P(("groups", "points"), None),
            P(("groups", "points"), None),
            P(("groups", "points"), None),
            P("groups"),
            P(("groups", "points", "centers"), None),
            P(("groups", "points", "centers"), None),
            P(("groups", "points", "centers")),
        ),
        out_specs=(
            P(("groups", "points", "centers"), None),
            P(("groups", "points", "centers"), None),
        ),
        check_vma=False,
    )
```

profile of v0, /device:TPU:0, one launch (start us, length us, event | category | flops | bytes accessed | tf_op | source)
XLA Modules:
  0.0 246.5 jit_solution(6114186068954046954)
XLA Ops:
  7.2 0.7 all-gather.3.cloned.1.call-update
  7.9 0.0 all-reduce.3.cloned.1.call-start
  8.0 0.7 reshape.29
  8.6 13.5 %all-gather = bf16[4,1,512]{2,1,0:T(2,128)(2,1)S(1)} all-gather(bf16[1,1,512]{2,1,0:T(2,128)(2,1)S(1)} %reshape.29), channel_id=1, replica_groups=mesh['groups'=2,'points'=4,'centers'=4] {'points'}, dimensions={0}, use_global_device_ids=true | all-gather | bytes 5120 | tf_op jit(solution)/shard_map/all_gather | solution.py:12
  22.2 22.0 %all_gather.11 = bf16[2048,128]{1,0:T(8,128)(2,1)} all-gather(bf16[512,128]{1,0:T(8,128)(2,1)} %param.18), channel_id=1, replica_groups=mesh['groups'=2,'points'=4,'centers'=4] {'points'}, dimensions={0}, use_global_device_ids=true | all-gather | bytes 655360 | tf_op jit(solution)/shard_map/all_gather | solution.py:11
  44.2 22.4 %all-gather.3.cloned.1.call-done = bf16[2048,512]{1,0:T(8,128)(2,1)} async-done(((bf16[512,512]{1,0:T(8,128)(2,1)}), bf16[2048,512]{1,0:T(8,128)(2,1)}) %all-gather.3.cloned.1.call-update) | async-done | bytes 2097168 | tf_op jit(solution)/shard_map/all_gather | solution.py:10
  66.5 2.1 multiply_reduce_fusion.1
  68.6 11.9 %while.36 = (s32[]{:T(128)}, bf16[2,512,2048]{2,1,0:T(8,128)(2,1)}, f32[1,2048]{1,0:T(1,128)S(1)}, bf16[2,512,512]{2,1,0:T(8,128)(2,1)}, f32[2048]{0:T(1024)S(1)}, /*index=5*/bf16[2048,512]{1,0:T(8,128)(2,1)}, s32[]{:T(128)}) while((s32[]{:T(128)}, bf16[2,512,2048]{2,1,0:T(8,128)(2,1)}, f32[1,2048]{1,0:T(1,128)S(1)}, ...), condition=%wide.region_3.4_spmd, body=%wide.region_1.3_spmd.sunk | while | flops 1080819200 | bytes 5264465 | solution.py:30
  68.6 1.2 multiply_reduce_fusion.3
  69.8 4.7 %fusion.33 = bf16[2,512,2048]{2,1,0:T(8,128)(2,1)} fusion(bf16[2,512,2048]{2,1,0:T(8,128)(2,1)} %get-tuple-element.330, s32[]{:T(128)} %get-tuple-element.329, bf16[2048,512]{1,0:T(8,128)(2,1)} %get-tuple-element.341, f32[2048]{0:T(1024)S(1)} %get-tuple-element.340, f32[512]{0:T(512)S(1)} %multiply_reduce_fusion.3, f32[2048]{0:T(1024)S(1)} %bitcast.62, ...), kind=kOutput, calls=%fused_computation.2.clone.1 | convolution fusion | flops 1080033280 | bytes 4738048 | tf_op jit(solution)/shard_map/while/body/eval_jaxpr/dot_general | solution.py:24
  74.5 1.2 multiply_reduce_fusion.3
  75.7 4.7 %fusion.33 = bf16[2,512,2048]{2,1,0:T(8,128)(2,1)} fusion(bf16[2,512,2048]{2,1,0:T(8,128)(2,1)} %get-tuple-element.330, s32[]{:T(128)} %get-tuple-element.329, bf16[2048,512]{1,0:T(8,128)(2,1)} %get-tuple-element.341, f32[2048]{0:T(1024)S(1)} %get-tuple-element.340, f32[512]{0:T(512)S(1)} %multiply_reduce_fusion.3, f32[2048]{0:T(1024)S(1)} %bitcast.62, ...), kind=kOutput, calls=%fused_computation.2.clone.1 | convolution fusion | flops 1080033280 | bytes 4738048 | tf_op jit(solution)/shard_map/while/body/eval_jaxpr/dot_general | solution.py:24
  80.5 4.5 %fusion.17 = f32[1024,128]{1,0:T(8,128)} fusion(bf16[1024,2048]{1,0:T(8,128)(2,1)} %bitcast.58, bf16[2048,128]{1,0:T(8,128)(2,1)} %all_gather.11), kind=kOutput, calls=%fused_computation.29 | convolution fusion | flops 536870912 | bytes 5242880 | tf_op jit(solution)/shard_map/dot_general | solution.py:31
  85.0 0.0 reduce-scatter.3.cloned.1.call-start
  85.1 32.1 %all-reduce.3.cloned.1.call-done = f32[1024,128]{1,0:T(8,128)} async-done(((f32[1024,128]{1,0:T(8,128)}), f32[1024,128]{1,0:T(8,128)}) %all-reduce.3.cloned.1.call-update) | async-done | bytes 524304 | tf_op jit(solution)/shard_map/psum | solution.py:34
  117.1 1.2 multiply_convert_fusion
  118.3 13.7 %while.37 = (s32[]{:T(128)}, f32[2048,512]{1,0:T(8,128)}, f32[2048]{0:T(1024)S(1)}, bf16[2,512,2048]{2,1,0:T(8,128)(2,1)}, bf16[2,512,128]{2,1,0:T(8,128)(2,1)S(...) while((s32[]{:T(128)}, f32[2048,512]{1,0:T(8,128)}, ...), condition=%wide.region_7.8_spmd.clone, body=%wide.region_5.7_spmd.clone.sunk | while | flops 1349519360 | bytes 15893612 | solution.py:74
  118.3 2.5 %convert_reduce_fusion.2 = (f32[2048]{0:T(1024)S(1)}, bf16[512,2048]{1,0:T(8,128)(2,1)S(1)}) fusion(bf16[2048,128]{1,0:T(8,128)(2,1)} %get-tuple-element.366, bf16[2,512,128]{2,1,0:T(8,128)(2,1)S(1)} %get-tuple-element.365, s32[]{:T(128)} %get-tuple-element.352, bf16[2,512,2048]{2,1,0:T(8,128)(2,1)} %get-tuple-element.364), kind=kOutput, calls=%fused_computation.10.clone.1 | convolution fusion | flops 273676288 | bytes 4858880 | tf_op jit(solution)/shard_map/while/body/eval_jaxpr/dot_general | solution.py:47
  120.8 3.2 %select_add_fusion.4 = f32[2048,512]{1,0:T(8,128)} fusion(f32[2048,512]{1,0:T(8,128)} %get-tuple-element.353, bf16[512,2048]{1,0:T(8,128)(2,1)S(1)} %get-tuple-element.316, pred[]{:T(512)S(6)} %compare.6, bf16[2,512,512]{2,1,0:T(8,128)(2,1)S(1)} %get-tuple-element.367, s32[]{:T(128)} %get-tuple-element.352), kind=kOutput, calls=%fused_computation.9.clone.1 | convolution fusion | flops 1075838976 | bytes 11010053 | tf_op jit(solution)/shard_map/while/body/eval_jaxpr/dot_general | solution.py:52
  124.1 2.5 %convert_reduce_fusion.2 = (f32[2048]{0:T(1024)S(1)}, bf16[512,2048]{1,0:T(8,128)(2,1)S(1)}) fusion(bf16[2048,128]{1,0:T(8,128)(2,1)} %get-tuple-element.366, bf16[2,512,128]{2,1,0:T(8,128)(2,1)S(1)} %get-tuple-element.365, s32[]{:T(128)} %get-tuple-element.352, bf16[2,512,2048]{2,1,0:T(8,128)(2,1)} %get-tuple-element.364), kind=kOutput, calls=%fused_computation.10.clone.1 | convolution fusion | flops 273676288 | bytes 4858880 | tf_op jit(solution)/shard_map/while/body/eval_jaxpr/dot_general | solution.py:47
  126.6 5.4 %select_add_fusion.4 = f32[2048,512]{1,0:T(8,128)} fusion(f32[2048,512]{1,0:T(8,128)} %get-tuple-element.353, bf16[512,2048]{1,0:T(8,128)(2,1)S(1)} %get-tuple-element.316, pred[]{:T(512)S(6)} %compare.6, bf16[2,512,512]{2,1,0:T(8,128)(2,1)S(1)} %get-tuple-element.367, s32[]{:T(128)} %get-tuple-element.352), kind=kOutput, calls=%fused_computation.9.clone.1 | convolution fusion | flops 1075838976 | bytes 11010053 | tf_op jit(solution)/shard_map/while/body/eval_jaxpr/dot_general | solution.py:52
  132.1 0.0 reduce-scatter.5.cloned.1.call-start
  132.2 5.4 %while.38 = (s32[]{:T(128)}, f32[2048,128]{1,0:T(8,128)S(1)}, bf16[2,512,2048]{2,1,0:T(8,128)(2,1)}, bf16[2,512,128]{2,1,0:T(8,128)(2,1)S(1)}, s32[]{:T(128)}, /*index=5*/s32[]{:T(128)}) while((s32[]{:T(128)}, f32[2048,128]{1,0:T(8,128)S(1)}, bf16[2,512,2048]{2,1,0:T(8,128)(2,1)}, bf16[2,512,128]{2,1,0:T(8,128)(2,1)S(1)}, ...), condition=%wide.region_11.12_spmd.clone, body=%wide.region_10.11_spmd.clone.sunk | while | flops 268959744 | bytes 4326479 | solution.py:65
  132.2 2.7 %convolution_add_fusion.2 = f32[2048,128]{1,0:T(8,128)S(1)} fusion(bf16[2,512,2048]{2,1,0:T(8,128)(2,1)} %get-tuple-element.384, s32[]{:T(128)} %get-tuple-element.376, f32[2048,128]{1,0:T(8,128)S(1)} %get-tuple-element.377, pred[]{:T(512)S(6)} %compare.7, bf16[2,512,128]{2,1,0:T(8,128)(2,1)S(1)} %get-tuple-element.385), kind=kOutput, calls=%fused_computation.18.clone.1 | convolution fusion | flops 268959744 | bytes 4326401 | tf_op jit(solution)/shard_map/while/body/eval_jaxpr/dot_general | solution.py:42
  134.9 2.6 %convolution_add_fusion.2 = f32[2048,128]{1,0:T(8,128)S(1)} fusion(bf16[2,512,2048]{2,1,0:T(8,128)(2,1)} %get-tuple-element.384, s32[]{:T(128)} %get-tuple-element.376, f32[2048,128]{1,0:T(8,128)S(1)} %get-tuple-element.377, pred[]{:T(512)S(6)} %compare.7, bf16[2,512,128]{2,1,0:T(8,128)(2,1)S(1)} %get-tuple-element.385), kind=kOutput, calls=%fused_computation.18.clone.1 | convolution fusion | flops 268959744 | bytes 4326401 | tf_op jit(solution)/shard_map/while/body/eval_jaxpr/dot_general | solution.py:42
  137.6 1.0 copy-done
  138.6 0.6 dynamic-slice
  139.8 12.4 %all-reduce = f32[2048]{0:T(1024)S(1)} all-reduce(f32[2048]{0:T(1024)S(1)} %get-tuple-element.136), channel_id=3, replica_groups=mesh['groups'=2,'points'=4,'centers'=4] {'points'}, use_global_device_ids=true, to_apply=%region_9.10.clone | all-reduce | flops 2048 | bytes 16384
  152.2 0.1 dynamic-slice.1
  152.3 57.2 %reduce-scatter.3.cloned.1.call-done = f32[512,512]{1,0:T(8,128)} async-done(((f32[2048,512]{1,0:T(8,128)}), f32[512,512]{1,0:T(8,128)}) %reduce-scatter.3.cloned.1.call-update) | async-done | bytes 1048592 | tf_op jit(solution)/shard_map/reduce_scatter | solution.py:78
  209.5 2.4 subtract_multiply_fusion
  211.9 28.1 %reduce-scatter.5.cloned.1.call-done = f32[512,128]{1,0:T(8,128)} async-done(((f32[2048,128]{1,0:T(8,128)}), f32[512,128]{1,0:T(8,128)}) %reduce-scatter.5.cloned.1.call-update) | async-done | bytes 262160 | tf_op jit(solution)/shard_map/reduce_scatter | solution.py:66
  (27 shorter events, 0.2 us)
Async XLA Ops:
  7.2 59.4 %all-gather.3.cloned.1.call-start = ((), (), s32[]{:S(2)}) async-start(), calls=%async_computation.2 | async-start | bytes 2621440 | tf_op jit(solution)/shard_map/all_gather | solution.py:10
  7.9 109.2 %all-reduce.3.cloned.1.call-start = ((), (), s32[]{:S(2)}) async-start(), calls=%async_computation.3 | async-start | bytes 1048576 | tf_op jit(solution)/shard_map/psum | solution.py:34
  80.5 36.7 %copy-start.3 = (f32[1024,128]{1,0:T(8,128)S(1)}, f32[1024,128]{1,0:T(8,128)}, u32[]{:S(2)}) copy-start(f32[1024,128]{1,0:T(8,128)} %param.15) | copy-start | bytes 1572868
  80.5 36.7 %copy-start.4 = (f32[1024,128]{1,0:T(8,128)S(1)}, f32[1024,128]{1,0:T(8,128)}, u32[]{:S(2)}) copy-start(f32[1024,128]{1,0:T(8,128)} %param.14) | copy-start | bytes 1572868
  80.5 36.7 %copy-start.6 = (f32[128]{0:T(128)S(1)}, f32[128]{0:T(128)}, u32[]{:S(2)}) copy-start(f32[128]{0:T(128)} %param.16) | copy-start | bytes 1540
  80.5 37.8 %copy-start.1 = (bf16[2,512,512]{2,1,0:T(8,128)(2,1)S(1)}, bf16[2,512,512]{2,1,0:T(8,128)(2,1)}, u32[]{:S(2)}) copy-start(bf16[2,512,512]{2,1,0:T(8,128)(2,1)} %get-tuple-element.397) | copy-start | bytes 3145732
  85.0 124.5 %reduce-scatter.3.cloned.1.call-start = ((), (), s32[]{:S(2)}) async-start(), calls=%async_computation.4 | async-start | bytes 5242880 | tf_op jit(solution)/shard_map/reduce_scatter | solution.py:78
  132.1 108.0 %reduce-scatter.5.cloned.1.call-start = ((), (), s32[]{:S(2)}) async-start(), calls=%async_computation.5 | async-start | bytes 1310720 | tf_op jit(solution)/shard_map/reduce_scatter | solution.py:66
  132.1 6.4 %copy-start.7 = (u32[32]{0:T(128)S(1)}, u32[32]{0:T(128)}, u32[]{:S(2)}) copy-start(u32[32]{0:T(128)} %constant.66) | copy-start | bytes 388
  132.1 7.7 %copy-start.5 = (bf16[512]{0:T(512)(128)(2,1)S(1)}, bf16[512]{0:T(512)(128)(2,1)}, u32[]{:S(2)}) copy-start(bf16[512]{0:T(512)(128)(2,1)} %param.19) | copy-start | bytes 3076
  132.1 77.4 %copy-start.2 = (bf16[512,512]{1,0:T(8,128)(2,1)S(1)}, bf16[512,512]{1,0:T(8,128)(2,1)}, u32[]{:S(2)}) copy-start(bf16[512,512]{1,0:T(8,128)(2,1)} %param.17) | copy-start | bytes 1572868
  137.5 1.0 copy-start
Sparse Core Ops, SparseCore 0:
  9.6 56.9 all-gather.2
  85.1 31.9 all-reduce.2
  132.2 77.2 reduce-scatter.2
  212.3 27.6 reduce-scatter.4
where the time goes:
time: 247 us
  waiting for transfers between devices  140 us (57%)
  blocking collectives  47.9 us (19%)
  matrix products  32.9 us (13%)
  between operations  14.6 us (6%)
  other arithmetic  8.14 us (3%)
    reduce_scatter x1, waiting for transfers between devices, per_device(): lax.psum_scatter(moment_acc, 'points', scatter_dimension=0, tiled=True)  57.2 us
    psum x1, waiting for transfers between devices, per_device(): panel_pred = lax.psum(partial_pred, 'centers')  32.1 us
    reduce_scatter x1, waiting for transfers between devices, per_device(): lax.psum_scatter(coef_acc, 'points', scatter_dimension=0, tiled=True)  28.1 us
    all_gather x1, waiting for transfers between devices, per_device(): lax.all_gather(center_pos, 'points', axis=0, tiled=True)  22.4 us
    all_gather x1, blocking collectives, per_device(): lax.all_gather(coefficients, 'points', axis=0, tiled=True)  22 us
    all_gather x1, blocking collectives, per_device(): lax.all_gather(spread, 'points', axis=0, tiled=True)  13.5 us
    unnamed x1, blocking collectives  12.4 us
    dot_general x2, matrix products, kernel_of(): lax.dot_general(row_block, whole_pos, (((1,), (1,)), ((), ())), preferred...  9.42 us
  transfers between devices with their start and end apart: 4, of which 4 were waited for; matrix products, arithmetic and copies ran while one was open for 4% of the time, Pallas kernels for 0%

commit v1 on v0

--- a/solution.py
+++ b/solution.py
@@ -31,7 +31,7 @@
     partial_pred = jnp.dot(
         kernels.reshape(n_points, panel_width), whole_coef, preferred_element_type=jnp.float32
     )
-    panel_pred = lax.psum(partial_pred, "centers")
+    panel_pred = jnp.sum(lax.all_gather(partial_pred, "centers"), axis=0)
     residual = panel_pred + saved_preds - targets
     cotangent = (residual / jnp.sqrt(1.0 + jnp.square(residual / huber_delta[None, :]))).astype(
         jnp.bfloat16

time: 247 us -> 237 us (0.960)
  waiting for transfers between devices: 140 us -> 130 us
    psum x1 -> x0, waiting for transfers between devices: 32.1 us -> none  [per_device(): panel_pred = lax.psum(partial_pred, 'centers')]
    all_gather x0 -> x1, waiting for transfers between devices: none -> 21.4 us  [per_device(): panel_pred = jnp.sum(lax.all_gather(partial_pred, 'centers'), axis=0)]
where the time goes in v1:
time: 237 us
  waiting for transfers between devices  130 us (55%)
  blocking collectives  47.8 us (20%)
  matrix products  32.9 us (14%)
  between operations  14.6 us (6%)
  other arithmetic  8.86 us (4%)
    reduce_scatter x1, waiting for transfers between devices, per_device(): lax.psum_scatter(moment_acc, 'points', scatter_dimension=0, tiled=True)  57.3 us
    reduce_scatter x1, waiting for transfers between devices, per_device(): lax.psum_scatter(coef_acc, 'points', scatter_dimension=0, tiled=True)  28.1 us
    all_gather x1, waiting for transfers between devices, per_device(): lax.all_gather(center_pos, 'points', axis=0, tiled=True)  22.4 us
    all_gather x1, blocking collectives, per_device(): lax.all_gather(coefficients, 'points', axis=0, tiled=True)  22 us
    all_gather x1, waiting for transfers between devices, per_device(): panel_pred = jnp.sum(lax.all_gather(partial_pred, 'centers'), axis=0)  21.4 us
    all_gather x1, blocking collectives, per_device(): lax.all_gather(spread, 'points', axis=0, tiled=True)  13.5 us
    unnamed x1, blocking collectives  12.3 us
    dot_general x2, matrix products, kernel_of(): lax.dot_general(row_block, whole_pos, (((1,), (1,)), ((), ())), preferred...  9.42 us
  transfers between devices with their start and end apart: 4, of which 4 were waited for; matrix products, arithmetic and copies ran while one was open for 4% of the time, Pallas kernels for 0%

profile of v1, /device:TPU:0, one launch (start us, length us, event | category | flops | bytes accessed | tf_op | source)
XLA Modules:
  0.0 236.7 jit_solution(12979579379665027416)
XLA Ops:
  7.2 0.7 all-gather.5.cloned.1.call-update
  8.0 0.7 reshape.30
  8.6 13.5 %all-gather.1 = bf16[4,1,512]{2,1,0:T(2,128)(2,1)S(1)} all-gather(bf16[1,1,512]{2,1,0:T(2,128)(2,1)S(1)} %reshape.30), channel_id=1, replica_groups=mesh['groups'=2,'points'=4,'centers'=4] {'points'}, dimensions={0}, use_global_device_ids=true | all-gather | bytes 5120 | tf_op jit(solution)/shard_map/all_gather | solution.py:12
  22.2 22.0 %all_gather.17 = bf16[2048,128]{1,0:T(8,128)(2,1)} all-gather(bf16[512,128]{1,0:T(8,128)(2,1)} %param.18), channel_id=1, replica_groups=mesh['groups'=2,'points'=4,'centers'=4] {'points'}, dimensions={0}, use_global_device_ids=true | all-gather | bytes 655360 | tf_op jit(solution)/shard_map/all_gather | solution.py:11
  44.2 22.4 %all-gather.5.cloned.1.call-done = bf16[2048,512]{1,0:T(8,128)(2,1)} async-done(((bf16[512,512]{1,0:T(8,128)(2,1)}), bf16[2048,512]{1,0:T(8,128)(2,1)}) %all-gather.5.cloned.1.call-update) | async-done | bytes 2097168 | tf_op jit(solution)/shard_map/all_gather | solution.py:10
  66.5 2.1 multiply_reduce_fusion.1
  68.6 11.9 %while.36 = (s32[]{:T(128)}, bf16[2,512,2048]{2,1,0:T(8,128)(2,1)}, f32[1,2048]{1,0:T(1,128)S(1)}, bf16[2,512,512]{2,1,0:T(8,128)(2,1)}, f32[2048]{0:T(1024)S(1)}, /*index=5*/bf16[2048,512]{1,0:T(8,128)(2,1)}, s32[]{:T(128)}) while((s32[]{:T(128)}, bf16[2,512,2048]{2,1,0:T(8,128)(2,1)}, f32[1,2048]{1,0:T(1,128)S(1)}, ...), condition=%wide.region_3.4_spmd, body=%wide.region_1.3_spmd.sunk | while | flops 1080819200 | bytes 5264465 | solution.py:30
  68.6 1.2 multiply_reduce_fusion.3
  69.8 4.7 %fusion.33 = bf16[2,512,2048]{2,1,0:T(8,128)(2,1)} fusion(bf16[2,512,2048]{2,1,0:T(8,128)(2,1)} %get-tuple-element.330, s32[]{:T(128)} %get-tuple-element.329, bf16[2048,512]{1,0:T(8,128)(2,1)} %get-tuple-element.341, f32[2048]{0:T(1024)S(1)} %get-tuple-element.340, f32[512]{0:T(512)S(1)} %multiply_reduce_fusion.3, f32[2048]{0:T(1024)S(1)} %bitcast.64, ...), kind=kOutput, calls=%fused_computation.2.clone.1 | convolution fusion | flops 1080033280 | bytes 4738048 | tf_op jit(solution)/shard_map/while/body/eval_jaxpr/dot_general | solution.py:24
  74.5 1.2 multiply_reduce_fusion.3
  75.7 4.7 %fusion.33 = bf16[2,512,2048]{2,1,0:T(8,128)(2,1)} fusion(bf16[2,512,2048]{2,1,0:T(8,128)(2,1)} %get-tuple-element.330, s32[]{:T(128)} %get-tuple-element.329, bf16[2048,512]{1,0:T(8,128)(2,1)} %get-tuple-element.341, f32[2048]{0:T(1024)S(1)} %get-tuple-element.340, f32[512]{0:T(512)S(1)} %multiply_reduce_fusion.3, f32[2048]{0:T(1024)S(1)} %bitcast.64, ...), kind=kOutput, calls=%fused_computation.2.clone.1 | convolution fusion | flops 1080033280 | bytes 4738048 | tf_op jit(solution)/shard_map/while/body/eval_jaxpr/dot_general | solution.py:24
  80.5 4.5 %fusion.17 = f32[1024,128]{1,0:T(8,128)} fusion(bf16[1024,2048]{1,0:T(8,128)(2,1)} %bitcast.59, bf16[2048,128]{1,0:T(8,128)(2,1)} %all_gather.17), kind=kOutput, calls=%fused_computation.29 | convolution fusion | flops 536870912 | bytes 5242880 | tf_op jit(solution)/shard_map/dot_general | solution.py:31
  85.0 0.0 reduce-scatter.3.cloned.1.call-start
  85.1 21.4 %all-gather.7.cloned.1.call-done = f32[4096,128]{1,0:T(8,128)} async-done(((f32[1024,128]{1,0:T(8,128)}), f32[4096,128]{1,0:T(8,128)}) %all-gather.7.cloned.1.call-update) | async-done | bytes 2097168 | tf_op jit(solution)/shard_map/all_gather | solution.py:34
  106.5 1.8 reduce_sum.39
  108.3 0.2 multiply_convert_fusion
  108.5 13.7 %while.37 = (s32[]{:T(128)}, f32[2048,512]{1,0:T(8,128)}, f32[2048]{0:T(1024)S(1)}, bf16[2,512,2048]{2,1,0:T(8,128)(2,1)}, bf16[2,512,128]{2,1,0:T(8,128)(2,1)S(...) while((s32[]{:T(128)}, f32[2048,512]{1,0:T(8,128)}, ...), condition=%wide.region_7.8_spmd.clone, body=%wide.region_5.7_spmd.clone.sunk | while | flops 1349519360 | bytes 15893612 | solution.py:74
  108.5 2.5 %convert_reduce_fusion.2 = (f32[2048]{0:T(1024)S(1)}, bf16[512,2048]{1,0:T(8,128)(2,1)S(1)}) fusion(bf16[2048,128]{1,0:T(8,128)(2,1)} %get-tuple-element.366, bf16[2,512,128]{2,1,0:T(8,128)(2,1)S(1)} %get-tuple-element.365, s32[]{:T(128)} %get-tuple-element.352, bf16[2,512,2048]{2,1,0:T(8,128)(2,1)} %get-tuple-element.364), kind=kOutput, calls=%fused_computation.10.clone.1 | convolution fusion | flops 273676288 | bytes 4858880 | tf_op jit(solution)/shard_map/while/body/eval_jaxpr/dot_general | solution.py:47
  111.0 3.2 %select_add_fusion.4 = f32[2048,512]{1,0:T(8,128)} fusion(f32[2048,512]{1,0:T(8,128)} %get-tuple-element.353, bf16[512,2048]{1,0:T(8,128)(2,1)S(1)} %get-tuple-element.316, pred[]{:T(512)S(6)} %compare.6, bf16[2,512,512]{2,1,0:T(8,128)(2,1)S(1)} %get-tuple-element.367, s32[]{:T(128)} %get-tuple-element.352), kind=kOutput, calls=%fused_computation.9.clone.1 | convolution fusion | flops 1075838976 | bytes 11010053 | tf_op jit(solution)/shard_map/while/body/eval_jaxpr/dot_general | solution.py:52
  114.2 2.5 %convert_reduce_fusion.2 = (f32[2048]{0:T(1024)S(1)}, bf16[512,2048]{1,0:T(8,128)(2,1)S(1)}) fusion(bf16[2048,128]{1,0:T(8,128)(2,1)} %get-tuple-element.366, bf16[2,512,128]{2,1,0:T(8,128)(2,1)S(1)} %get-tuple-element.365, s32[]{:T(128)} %get-tuple-element.352, bf16[2,512,2048]{2,1,0:T(8,128)(2,1)} %get-tuple-element.364), kind=kOutput, calls=%fused_computation.10.clone.1 | convolution fusion | flops 273676288 | bytes 4858880 | tf_op jit(solution)/shard_map/while/body/eval_jaxpr/dot_general | solution.py:47
  116.7 5.4 %select_add_fusion.4 = f32[2048,512]{1,0:T(8,128)} fusion(f32[2048,512]{1,0:T(8,128)} %get-tuple-element.353, bf16[512,2048]{1,0:T(8,128)(2,1)S(1)} %get-tuple-element.316, pred[]{:T(512)S(6)} %compare.6, bf16[2,512,512]{2,1,0:T(8,128)(2,1)S(1)} %get-tuple-element.367, s32[]{:T(128)} %get-tuple-element.352), kind=kOutput, calls=%fused_computation.9.clone.1 | convolution fusion | flops 1075838976 | bytes 11010053 | tf_op jit(solution)/shard_map/while/body/eval_jaxpr/dot_general | solution.py:52
  122.2 0.0 reduce-scatter.5.cloned.1.call-start
  122.3 5.4 %while.38 = (s32[]{:T(128)}, f32[2048,128]{1,0:T(8,128)S(1)}, bf16[2,512,2048]{2,1,0:T(8,128)(2,1)}, bf16[2,512,128]{2,1,0:T(8,128)(2,1)S(1)}, s32[]{:T(128)}, /*index=5*/s32[]{:T(128)}) while((s32[]{:T(128)}, f32[2048,128]{1,0:T(8,128)S(1)}, bf16[2,512,2048]{2,1,0:T(8,128)(2,1)}, bf16[2,512,128]{2,1,0:T(8,128)(2,1)S(1)}, ...), condition=%wide.region_11.12_spmd.clone, body=%wide.region_10.11_spmd.clone.sunk | while | flops 268959744 | bytes 4326479 | solution.py:65
  122.3 2.7 %convolution_add_fusion.2 = f32[2048,128]{1,0:T(8,128)S(1)} fusion(bf16[2,512,2048]{2,1,0:T(8,128)(2,1)} %get-tuple-element.384, s32[]{:T(128)} %get-tuple-element.376, f32[2048,128]{1,0:T(8,128)S(1)} %get-tuple-element.377, pred[]{:T(512)S(6)} %compare.7, bf16[2,512,128]{2,1,0:T(8,128)(2,1)S(1)} %get-tuple-element.385), kind=kOutput, calls=%fused_computation.18.clone.1 | convolution fusion | flops 268959744 | bytes 4326401 | tf_op jit(solution)/shard_map/while/body/eval_jaxpr/dot_general | solution.py:42
  125.0 2.6 %convolution_add_fusion.2 = f32[2048,128]{1,0:T(8,128)S(1)} fusion(bf16[2,512,2048]{2,1,0:T(8,128)(2,1)} %get-tuple-element.384, s32[]{:T(128)} %get-tuple-element.376, f32[2048,128]{1,0:T(8,128)S(1)} %get-tuple-element.377, pred[]{:T(512)S(6)} %compare.7, bf16[2,512,128]{2,1,0:T(8,128)(2,1)S(1)} %get-tuple-element.385), kind=kOutput, calls=%fused_computation.18.clone.1 | convolution fusion | flops 268959744 | bytes 4326401 | tf_op jit(solution)/shard_map/while/body/eval_jaxpr/dot_general | solution.py:42
  127.7 1.0 copy-done
  128.7 0.6 dynamic-slice
  129.9 12.3 %all-reduce = f32[2048]{0:T(1024)S(1)} all-reduce(f32[2048]{0:T(1024)S(1)} %get-tuple-element.136), channel_id=4, replica_groups=mesh['groups'=2,'points'=4,'centers'=4] {'points'}, use_global_device_ids=true, to_apply=%region_9.10.clone | all-reduce | flops 2048 | bytes 16384
  142.3 0.1 dynamic-slice.1
  142.4 57.3 %reduce-scatter.3.cloned.1.call-done = f32[512,512]{1,0:T(8,128)} async-done(((f32[2048,512]{1,0:T(8,128)}), f32[512,512]{1,0:T(8,128)}) %reduce-scatter.3.cloned.1.call-update) | async-done | bytes 1048592 | tf_op jit(solution)/shard_map/reduce_scatter | solution.py:78
  199.6 2.4 %subtract_multiply_fusion = f32[512,512]{1,0:T(8,128)} fusion(f32[512,512]{1,0:T(8,128)} %reduce-scatter.3.cloned.1.call-done, bf16[512,512]{1,0:T(8,128)(2,1)S(1)} %copy-done.2, f32[512]{0:T(512)S(1)} %dynamic-slice.1, f32[512]{0:T(512)S(1)} %convert_multiply_fusion.1), kind=kLoop, calls=%fused_computation.25 | loop fusion | flops 1048576 | bytes 2625536 | tf_op jit(solution)/shard_map/mul | solution.py:82
  202.1 28.1 %reduce-scatter.5.cloned.1.call-done = f32[512,128]{1,0:T(8,128)} async-done(((f32[2048,128]{1,0:T(8,128)}), f32[512,128]{1,0:T(8,128)}) %reduce-scatter.5.cloned.1.call-update) | async-done | bytes 262160 | tf_op jit(solution)/shard_map/reduce_scatter | solution.py:66
  (28 shorter events, 0.2 us)
Async XLA Ops:
  7.2 59.4 %all-gather.5.cloned.1.call-start = ((), (), s32[]{:S(2)}) async-start(), calls=%async_computation.2 | async-start | bytes 2621440 | tf_op jit(solution)/shard_map/all_gather | solution.py:10
  7.9 98.6 %all-gather.7.cloned.1.call-start = ((), (), s32[]{:S(2)}) async-start(), calls=%async_computation.5 | async-start | bytes 2621440 | tf_op jit(solution)/shard_map/all_gather | solution.py:34
  80.5 27.8 %copy-start.3 = (f32[1024,128]{1,0:T(8,128)S(1)}, f32[1024,128]{1,0:T(8,128)}, u32[]{:S(2)}) copy-start(f32[1024,128]{1,0:T(8,128)} %param.15) | copy-start | bytes 1572868
  80.5 27.8 %copy-start.4 = (f32[1024,128]{1,0:T(8,128)S(1)}, f32[1024,128]{1,0:T(8,128)}, u32[]{:S(2)}) copy-start(f32[1024,128]{1,0:T(8,128)} %param.14) | copy-start | bytes 1572868
  80.5 27.8 %copy-start.6 = (f32[128]{0:T(128)S(1)}, f32[128]{0:T(128)}, u32[]{:S(2)}) copy-start(f32[128]{0:T(128)} %param.16) | copy-start | bytes 1540
  80.5 28.0 %copy-start.1 = (bf16[2,512,512]{2,1,0:T(8,128)(2,1)S(1)}, bf16[2,512,512]{2,1,0:T(8,128)(2,1)}, u32[]{:S(2)}) copy-start(bf16[2,512,512]{2,1,0:T(8,128)(2,1)} %get-tuple-element.397) | copy-start | bytes 3145732
  85.0 114.7 %reduce-scatter.3.cloned.1.call-start = ((), (), s32[]{:S(2)}) async-start(), calls=%async_computation.3 | async-start | bytes 5242880 | tf_op jit(solution)/shard_map/reduce_scatter | solution.py:78
  122.2 108.0 %reduce-scatter.5.cloned.1.call-start = ((), (), s32[]{:S(2)}) async-start(), calls=%async_computation.4 | async-start | bytes 1310720 | tf_op jit(solution)/shard_map/reduce_scatter | solution.py:66
  122.3 6.4 %copy-start.7 = (u32[32]{0:T(128)S(1)}, u32[32]{0:T(128)}, u32[]{:S(2)}) copy-start(u32[32]{0:T(128)} %constant.66) | copy-start | bytes 388
  122.3 7.7 %copy-start.5 = (bf16[512]{0:T(512)(128)(2,1)S(1)}, bf16[512]{0:T(512)(128)(2,1)}, u32[]{:S(2)}) copy-start(bf16[512]{0:T(512)(128)(2,1)} %param.19) | copy-start | bytes 3076
  122.3 77.4 %copy-start.2 = (bf16[512,512]{1,0:T(8,128)(2,1)S(1)}, bf16[512,512]{1,0:T(8,128)(2,1)}, u32[]{:S(2)}) copy-start(bf16[512,512]{1,0:T(8,128)(2,1)} %param.17) | copy-start | bytes 1572868
  127.7 1.0 copy-start
Sparse Core Ops, SparseCore 0:
  9.6 56.9 all-gather.4
  85.1 21.3 all-gather.6
  122.3 77.2 reduce-scatter.2
  202.5 27.6 reduce-scatter.4
